TPU v7x, 256 devices: a whole 4x4x8 slice. The times are simulated.
256 devices in a mesh: grp: 8 (over z_hi, core), blk: 32 (over x, y, z_lo).
Axes of the slice: x: 4, y: 4, z: 8 (z_hi: 4, z_lo: 2; z = z_hi * 2 + z_lo), core: 2. Of those that a mesh axis runs over, the one named last changes fastest.
Arguments:
- factors: bfloat16 [1024, 512, 512], P(('grp', 'blk')), may hold values from -6 to 6
- loadings: bfloat16 [512, 2048], replicated, may hold values from -0.25 to 0.25
- netload_map: bfloat16 [512, 200], replicated, may hold values from -0.25 to 0.25
- rule_weights: bfloat16 [32, 2048, 200], P('blk'), may hold values from -0.125 to 0.125
- rule_bias: float32 [32, 200], P('blk'), may hold values from -3 to 3
Outputs:
- decisions: bfloat16 [512, 1024, 200], P('blk', 'grp')
- rule_grad: float32 [32, 2048, 200], P('blk', 'grp')
All inputs are finite; a program needn't handle non-finite values.
Results may differ from a plain program's by a relative error of at most 0.01.
Values may be sent and summed in bfloat16 or wider, within the bound.
A program may use at most 128 MiB of HBM per device.

v0:
```python
import math

import jax
import jax.numpy as jnp
from jax import lax
from jax.sharding import PartitionSpec as P


def body(factors, loadings, netload_map, rule_weights, rule_bias):
    blocks = lax.axis_size("blk")
    groups = lax.axis_size("grp")
    path_dev, hours, width_k = factors.shape
    hour_blk = hours // blocks
    row_scale = 1.0 / math.sqrt(groups * blocks * path_dev * hour_blk)
    weights = rule_weights[0]
    offsets = rule_bias[0]
    ordered = jnp.transpose(factors.reshape(path_dev, blocks, hour_blk, width_k), (1, 2, 0, 3))
    features = jnp.tanh(
        jnp.einsum("...c,cf->...f", ordered, loadings, preferred_element_type=jnp.float32)
    ).astype(jnp.bfloat16)
    net_load = jnp.einsum(
        "...c,cd->...d", ordered, netload_map, preferred_element_type=jnp.float32
    ).astype(jnp.bfloat16)
    features, net_load = (features, net_load)
    decide_features = lax.all_to_all(features, "blk", split_axis=0, concat_axis=2, tiled=True)[0]
    decide_net_load = lax.all_to_all(net_load, "blk", split_axis=0, concat_axis=2, tiled=True)[0]
    dispatch = (
        jnp.einsum("krf,fd->krd", decide_features, weights, preferred_element_type=jnp.float32)
        + offsets
    )
    shortfall = decide_net_load.astype(jnp.float32) - dispatch
    slopes = (
        -4.0 * jax.nn.sigmoid(shortfall) + jax.nn.sigmoid(-shortfall) + 0.25 * dispatch
    ).astype(jnp.bfloat16)
    decisions, slopes, received = (dispatch.astype(jnp.bfloat16), slopes, decide_features)
    partial_grad = (
        jnp.einsum("krf,krd->fd", received, slopes, preferred_element_type=jnp.float32) * row_scale
    )[None]
    summed = lax.psum(partial_grad.astype(jnp.bfloat16), "grp").astype(jnp.float32)
    owned = partial_grad.shape[1] // groups
    grad_share = lax.dynamic_slice_in_dim(summed, lax.axis_index("grp") * owned, owned, 1)
    return (decisions, grad_share)


def solution(mesh):
    return jax.shard_map(
        body,
        mesh=mesh,
        in_specs=(P(("grp", "blk"), None, None), P(), P(), P("blk", None, None), P("blk", None)),
        out_specs=(P("blk", "grp", None), P("blk", "grp", None)),
        check_vma=False,
    )
```

profile of v0, /device:TPU:1, one launch (start us, length us, event | category | flops | bytes accessed | tf_op | source)
XLA Modules:
  0.0 289.5 jit_solution(17951146941334778530)
XLA Ops:
  7.2 0.0 copy-start
  7.2 3.4 %fusion.9 = bf16[32,16,4,200]{3,1,2,0:T(8,128)(2,1)} fusion(bf16[4,32,16,512]{3,2,1,0:T(8,128)(2,1)} %bitcast.49, bf16[512,200]{0,1:T(8,128)(2,1)} %param.7), kind=kOutput, calls=%fused_computation.13 | convolution fusion | flops 419840000 | bytes 3121152 | tf_op jit(solution)/shard_map/...c,cd->...d/dot_general | solution.py:21
  10.6 9.2 %all-to-all-start.1 = ((bf16[32,16,4,200]{3,1,2,0:T(8,128)(2,1)}), bf16[32,16,4,200]{3,1,2,0:T(8,128)(2,1)S(1)}, u32[]{:S(2)}, u32[]{:S(2)}) async-start(bf16[32,16,4,200]{3,1,2,0:T(8,128)(2,1)} %fusion.9), calls=%async_computation.1 | async-start | bytes 2097152 | tf_op jit(solution)/shard_map/all_to_all | solution.py:26
  19.8 0.0 copy-done
  19.8 8.3 %tanh_convert_fusion = bf16[32,16,4,2048]{3,1,2,0:T(8,128)(2,1)} fusion(bf16[512,2048]{1,0:T(8,128)(2,1)S(1)} %copy-done, bf16[4,32,16,512]{3,2,1,0:T(8,128)(2,1)} %bitcast.50), kind=kOutput, calls=%fused_computation | convolution fusion | flops 4299161600 | bytes 12582912 | tf_op jit(solution)/shard_map/...c,cf->...f/dot_general | solution.py:19
  28.2 8.4 %all-to-all-done.1 = bf16[32,16,4,200]{3,1,2,0:T(8,128)(2,1)S(1)} async-done(((bf16[32,16,4,200]{3,1,2,0:T(8,128)(2,1)}), bf16[32,16,4,200]{3,1,2,0:T(8,128)(2,1)S(1)}, u32[]{:S(2)}, u32[]{:S(2)}) %all-to-all-start.1) | async-done | bytes 819232 | tf_op jit(solution)/shard_map/all_to_all | solution.py:26
  36.6 5.0 %all-to-all-start = ((bf16[32,16,4,2048]{3,1,2,0:T(8,128)(2,1)}), bf16[32,16,4,2048]{3,1,2,0:T(8,128)(2,1)}, u32[]{:S(2)}, u32[]{:S(2)}) async-start(bf16[32,16,4,2048]{3,1,2,0:T(8,128)(2,1)} %tanh_convert_fusion), calls=%async_computation | async-start | bytes 16777216 | tf_op jit(solution)/shard_map/all_to_all | solution.py:25
  41.5 0.0 all-reduce.2.cloned.1.call-start
  41.6 1.6 bitcast_convert_fusion
  43.2 0.0 copy-start.2
  43.2 2.9 %copy.13 = f32[16,128,200]{1,2,0:T(8,128)} copy(f32[16,128,200]{2,0,1:T(8,128)} %bitcast.47) | data formatting | bytes 3276800 | tf_op jit(solution)/shard_map/convert_element_type | solution.py:31
  46.2 129.4 %all-to-all-done = bf16[32,16,4,2048]{3,1,2,0:T(8,128)(2,1)} async-done(((bf16[32,16,4,2048]{3,1,2,0:T(8,128)(2,1)}), bf16[32,16,4,2048]{3,1,2,0:T(8,128)(2,1)}, u32[]{:S(2)}, u32[]{:S(2)}) %all-to-all-start) | async-done | bytes 8388640 | tf_op jit(solution)/shard_map/all_to_all | solution.py:25
  175.6 0.0 copy-done.2
  175.6 7.1 %fusion.12 = f32[16,128,200]{2,0,1:T(8,128)} fusion(bf16[16,128,2048]{2,0,1:T(8,128)(2,1)} %bitcast.6, bf16[1,2048,200]{1,2,0:T(8,128)(2,1)S(1)} %copy-done.2), kind=kOutput, calls=%fused_computation.15 | convolution fusion | flops 1677721600 | bytes 10846208 | tf_op jit(solution)/shard_map/krf,fd->krd/dot_general | solution.py:28
  182.7 0.0 copy-start.1
  182.7 2.9 copy.17
  185.6 0.0 copy-done.1
  185.6 3.7 %add_convert_fusion = (bf16[16,128,200]{1,2,0:T(8,128)(2,1)S(1)}, bf16[16,128,200]{1,2,0:T(8,128)(2,1)}) fusion(f32[16,128,200]{1,2,0:T(8,128)} %copy.13, f32[16,128,200]{1,2,0:T(8,128)} %copy.17, f32[200]{0:T(256)S(1)} %bitcast.48), kind=kLoop, calls=%fused_computation.11 | loop fusion | flops 5324800 | bytes 4916000 | tf_op jit(solution)/shard_map/convert_element_type | solution.py:34
  189.3 1.7 copy.20
  191.0 6.4 %fusion.2 = bf16[1,2048,200]{1,2,0:T(8,128)(2,1)} fusion(bf16[16,128,2048]{2,0,1:T(8,128)(2,1)} %bitcast.6, bf16[16,128,200]{2,0,1:T(8,128)(2,1)} %copy.20), kind=kOutput, calls=%fused_computation.4 | convolution fusion | flops 1678540800 | bytes 10027008 | tf_op jit(solution)/shard_map/krf,krd->fd/dot_general | solution.py:37
  197.4 0.0 all-reduce.2.cloned.1.call-update
  197.4 83.7 %all-reduce.2.cloned.1.call-done = bf16[1,2048,200]{1,2,0:T(8,128)(2,1)} async-done(((bf16[1,2048,200]{1,2,0:T(8,128)(2,1)}), bf16[1,2048,200]{1,2,0:T(8,128)(2,1)}) %all-reduce.2.cloned.1.call-update) | async-done | bytes 819216 | tf_op jit(solution)/shard_map/psum | solution.py:39
  281.1 1.6 dynamic-slice_convert_fusion
Async XLA Ops:
  7.2 12.7 %copy-start = (bf16[512,2048]{1,0:T(8,128)(2,1)S(1)}, bf16[512,2048]{1,0:T(8,128)(2,1)}, u32[]{:S(2)}) copy-start(bf16[512,2048]{1,0:T(8,128)(2,1)} %param.6) | copy-start | bytes 6291460
  10.6 25.9 %all-to-all-start.1 = ((bf16[32,16,4,200]{3,1,2,0:T(8,128)(2,1)}), bf16[32,16,4,200]{3,1,2,0:T(8,128)(2,1)S(1)}, u32[]{:S(2)}, u32[]{:S(2)}) async-start(bf16[32,16,4,200]{3,1,2,0:T(8,128)(2,1)} %fusion.9), calls=%async_computation.1 | async-start | bytes 2097152 | tf_op jit(solution)/shard_map/all_to_all | solution.py:26
  36.6 139.0 %all-to-all-start = ((bf16[32,16,4,2048]{3,1,2,0:T(8,128)(2,1)}), bf16[32,16,4,2048]{3,1,2,0:T(8,128)(2,1)}, u32[]{:S(2)}, u32[]{:S(2)}) async-start(bf16[32,16,4,2048]{3,1,2,0:T(8,128)(2,1)} %tanh_convert_fusion), calls=%async_computation | async-start | bytes 16777216 | tf_op jit(solution)/shard_map/all_to_all | solution.py:25
  41.5 239.6 %all-reduce.2.cloned.1.call-start = ((), (), s32[]{:S(2)}) async-start(), calls=%async_computation.2 | async-start | bytes 1638400 | tf_op jit(solution)/shard_map/psum | solution.py:39
  43.2 132.4 %copy-start.2 = (bf16[1,2048,200]{1,2,0:T(8,128)(2,1)S(1)}, bf16[1,2048,200]{1,2,0:T(8,128)(2,1)}, u32[]{:S(2)}) copy-start(bf16[1,2048,200]{1,2,0:T(8,128)(2,1)} %param.8) | copy-start | bytes 2457604
  182.7 2.9 copy-start.1
Sparse Core Ops, SparseCore 0:
  197.5 83.5 all-reduce.1
where the time goes:
time: 290 us
  waiting for transfers between devices  222 us (77%)
  matrix products  25.3 us (9%)
  starting transfers between devices  14.2 us (5%)
  between operations  14.1 us (5%)
  local copies, waits for them, and re-layouts  7.5 us (3%)
  other arithmetic  6.93 us (2%)
    all_to_all x1, waiting for transfers between devices, body(): lax.all_to_all(features, 'blk', split_axis=0, concat_axis=2, tiled=True)[0]  129 us
    psum x1, waiting for transfers between devices, body(): lax.psum(partial_grad.astype(jnp.bfloat16), 'grp').astype(jnp.float32)  83.7 us
    all_to_all x1, starting transfers between devices, body(): lax.all_to_all(net_load, 'blk', split_axis=0, concat_axis=2, tiled=True)[0]  9.21 us
    all_to_all x1, waiting for transfers between devices, body(): lax.all_to_all(net_load, 'blk', split_axis=0, concat_axis=2, tiled=True)[0]  8.41 us
    dot_general x1, matrix products, body(): jnp.einsum('...c,cf->...f', ordered, loadings, preferred_element_type=jnp...  8.32 us
    dot_general x1, matrix products, body(): jnp.einsum('krf,fd->krd', decide_features, weights, preferred_element_typ...  7.12 us
    dot_general x1, matrix products, body(): jnp.einsum('krf,krd->fd', received, slopes, preferred_element_type=jnp.fl...  6.41 us
  transfers between devices with their start and end apart: 3, of which 3 were waited for; matrix products, arithmetic and copies ran while one was open for 4% of the time, Pallas kernels for 0%

commit v1 on v0

v1 whole, which is shorter than its diff:
```python
import math

import jax
import jax.numpy as jnp
from jax import lax
from jax.sharding import PartitionSpec as P


def body(factors, loadings, netload_map, rule_weights, rule_bias):
    blocks = lax.axis_size("blk")
    groups = lax.axis_size("grp")
    path_dev, hours, width_k = factors.shape
    hour_blk = hours // blocks
    row_scale = 1.0 / math.sqrt(groups * blocks * path_dev * hour_blk)
    weights = rule_weights[0]
    offsets = rule_bias[0]
    ordered = factors.reshape(path_dev, blocks, hour_blk, width_k)
    shocks = lax.all_to_all(ordered, "blk", split_axis=1, concat_axis=0, tiled=True)
    shocks = shocks.reshape(blocks * path_dev, hour_blk, width_k)
    features = jnp.tanh(
        jnp.einsum("rkc,cf->rkf", shocks, loadings, preferred_element_type=jnp.float32)
    ).astype(jnp.bfloat16)
    net_load = jnp.einsum(
        "rkc,cd->rkd", shocks, netload_map, preferred_element_type=jnp.float32
    ).astype(jnp.bfloat16)
    dispatch = (
        jnp.einsum("rkf,fd->rkd", features, weights, preferred_element_type=jnp.float32)
        + offsets
    )
    shortfall = net_load.astype(jnp.float32) - dispatch
    slopes = (
        -4.0 * jax.nn.sigmoid(shortfall) + jax.nn.sigmoid(-shortfall) + 0.25 * dispatch
    ).astype(jnp.bfloat16)
    decisions = jnp.transpose(dispatch.astype(jnp.bfloat16), (1, 0, 2))
    partial_grad = (
        jnp.einsum("rkf,rkd->fd", features, slopes, preferred_element_type=jnp.float32) * row_scale
    ).astype(jnp.bfloat16)
    grad_share = lax.psum_scatter(partial_grad, "grp", scatter_dimension=0, tiled=True)
    return (decisions, grad_share.astype(jnp.float32)[None])


def solution(mesh):
    return jax.shard_map(
        body,
        mesh=mesh,
        in_specs=(P(("grp", "blk"), None, None), P(), P(), P("blk", None, None), P("blk", None)),
        out_specs=(P("blk", "grp", None), P("blk", "grp", None)),
        check_vma=False,
    )
```

time: 290 us -> 119 us (0.41)
  waiting for transfers between devices: 222 us -> 34.8 us
  blocking collectives: 0 us -> 37.1 us
  starting transfers between devices: 14.2 us -> 0.04 us
  matrix products: 25.3 us -> 18.5 us
    all_to_all x2 -> x0, waiting for transfers between devices: 138 us -> none  [the longest x1 129 us: body(): lax.all_to_all(features, 'blk', split_axis=0, concat_axis=2, tiled=True)[0]]
    psum x1 -> x0, waiting for transfers between devices: 83.7 us -> none  [body(): lax.psum(partial_grad.astype(jnp.bfloat16), 'grp').astype(jnp.float32)]
    all_to_all x0 -> x1, blocking collectives: none -> 37.1 us  [body(): lax.all_to_all(ordered, 'blk', split_axis=1, concat_axis=0, tiled=True)]
    reduce_scatter x0 -> x1, waiting for transfers between devices: none -> 34.8 us  [body(): lax.psum_scatter(partial_grad, 'grp', scatter_dimension=0, tiled=True)]
    all_to_all x2 -> x0, starting transfers between devices: 14.2 us -> none  [the longest x1 9.21 us: body(): lax.all_to_all(net_load, 'blk', split_axis=0, concat_axis=2, tiled=True)[0]]
    dot_general x4 -> x3, matrix products: 25.3 us -> 18.5 us  [the longest x1 8.15 us: body(): jnp.einsum('rkf,rkd->fd', features, slopes, preferred_element_type=jnp.fl...]
    convert_element_type x2 -> x0, local copies, waits for them, and re-layouts: 4.62 us -> none  [the longest x1 2.94 us: body(): shortfall = decide_net_load.astype(jnp.float32) - dispatch]
    convert_element_type x3 -> x1, other arithmetic: 6.93 us -> 2.52 us  [body(): decisions = jnp.transpose(dispatch.astype(jnp.bfloat16), (1, 0, 2))]
  transfers between devices with their start and end apart: 3 -> 1, of which waited for: 3 -> 1; matrix products, arithmetic and copies ran while one was open for 4% -> 2% of each run, Pallas kernels for 0% -> 0%
where the time goes in v1:
time: 119 us; the launch traced here: 118 us
  blocking collectives  37.1 us (31%)
  waiting for transfers between devices  34.8 us (29%)
  matrix products  18.5 us (16%)
  between operations  14.1 us (12%)
  local copies, waits for them, and re-layouts  9.72 us (8%)
  other arithmetic  4.11 us (3%)
    all_to_all x1, blocking collectives, body(): lax.all_to_all(ordered, 'blk', split_axis=1, concat_axis=0, tiled=True)  37.1 us
    reduce_scatter x1, waiting for transfers between devices, body(): lax.psum_scatter(partial_grad, 'grp', scatter_dimension=0, tiled=True)  34.8 us
    dot_general x1, matrix products, body(): jnp.einsum('rkf,rkd->fd', features, slopes, preferred_element_type=jnp.fl...  8.15 us
    dot_general x1, matrix products, body(): jnp.einsum('rkc,cf->rkf', shocks, loadings, preferred_element_type=jnp.fl...  6.38 us
    dot_general x1, matrix products, body(): jnp.einsum('rkf,fd->rkd', features, weights, preferred_element_type=jnp.f...  4.01 us
    reshape x1, local copies, waits for them, and re-layouts, body(): shocks = shocks.reshape(blocks * path_dev, hour_blk, width_k)  3.98 us
    unnamed x11, local copies, waits for them, and re-layouts  3.38 us
    convert_element_type x1, other arithmetic, body(): decisions = jnp.transpose(dispatch.astype(jnp.bfloat16), (1, 0, 2))  2.52 us
  transfers between devices with their start and end apart: 1, of which 1 were waited for; matrix products, arithmetic and copies ran while one was open for 2% of the time, Pallas kernels for 0%

profile of v1, /device:TPU:1, one launch (start us, length us, event | category | flops | bytes accessed | tf_op | source)
XLA Modules:
  0.0 118.4 jit_solution(18331802904006783247)
XLA Ops:
  7.2 0.0 copy-start
  7.2 0.0 reduce-scatter.2.cloned.1.call-start
  7.2 3.4 %copy.8 = bf16[4,512,512]{2,0,1:T(4,128)(2,1)S(1)} copy(bf16[4,512,512]{2,1,0:T(8,128)(2,1)} %param.5) | data formatting | bytes 4194304 | tf_op args[0]
  10.6 37.1 %all_to_all.15 = bf16[4,32,16,512]{3,0,2,1:T(4,128)(2,1)S(1)} all-to-all(bf16[4,32,16,512]{3,0,2,1:T(4,128)(2,1)S(1)} %bitcast.34), channel_id=1, replica_groups=mesh['grp'=8,'blk'=32] {'blk'}, dimensions={1} | all-to-all | bytes 4194304 | tf_op jit(solution)/shard_map/all_to_all | solution.py:18
  47.6 2.4 %copy.9 = bf16[32,4,1,16,512]{4,1,0,3,2:T(4,128)(2,1)} copy(bf16[32,4,1,16,512]{4,1,3,0,2:T(4,128)(2,1)S(1)} %bitcast.33) | data formatting | bytes 4194304 | tf_op jit(solution)/shard_map/all_to_all | solution.py:18
  50.0 4.0 %reshape.13 = bf16[128,16,512]{2,0,1:T(8,128)(2,1)} reshape(bf16[32,4,1,16,512]{4,1,0,3,2:T(4,128)(2,1)} %copy.9) | data formatting | bytes 4194304 | tf_op jit(solution)/shard_map/reshape | solution.py:19
  54.0 0.0 copy-done
  54.0 0.0 copy-start.2
  54.0 6.4 %tanh_convert_fusion = bf16[128,16,2048]{2,0,1:T(8,128)(2,1)S(1)} fusion(bf16[128,16,512]{2,0,1:T(8,128)(2,1)} %reshape.13, bf16[512,2048]{1,0:T(8,128)(2,1)S(1)} %copy-done), kind=kOutput, calls=%fused_computation | convolution fusion | flops 4299161600 | bytes 12582912 | tf_op jit(solution)/shard_map/rkc,cf->rkf/dot_general | solution.py:21
  60.4 0.0 copy-done.2
  60.4 0.0 copy-start.4
  60.4 0.0 copy-start.1
  60.4 0.0 copy-start.3
  60.4 4.0 %fusion.4 = f32[128,16,200]{0,2,1:T(8,128)} fusion(bf16[128,16,2048]{2,0,1:T(8,128)(2,1)S(1)} %tanh_convert_fusion, bf16[1,2048,200]{1,2,0:T(8,128)(2,1)S(1)} %copy-done.2), kind=kOutput, calls=%fused_computation.9 | convolution fusion | flops 1677721600 | bytes 10846208 | tf_op jit(solution)/shard_map/rkf,fd->rkd/dot_general | solution.py:27
  64.4 0.0 copy-done.4
  64.4 0.0 copy-done.1
  64.4 0.0 copy-done.3
  64.4 8.2 %fusion.1 = bf16[2048,200]{0,1:T(8,128)(2,1)} fusion(bf16[128,16,2048]{2,0,1:T(8,128)(2,1)} %copy-done.4, f32[128,16,200]{0,2,1:T(8,128)} %fusion.4, bf16[128,16,512]{2,0,1:T(8,128)(2,1)} %reshape.13, f32[200]{0:T(256)S(1)} %bitcast.35, bf16[512,200]{0,1:T(8,128)(2,1)S(1)} %copy-done.3), kind=kOutput, calls=%fused_computation.3 | convolution fusion | flops 2103705600 | bytes 13148960 | tf_op jit(solution)/shard_map/rkf,rkd->fd/dot_general | solution.py:36
  72.6 0.0 reduce-scatter.2.cloned.1.call-update
  72.6 2.5 %fusion.3 = bf16[16,128,200]{1,2,0:T(8,128)(2,1)} fusion(f32[128,16,200]{0,2,1:T(8,128)} %fusion.4, f32[200]{0:T(256)S(1)} %bitcast.36), kind=kLoop, calls=%fused_computation.8 | loop fusion | flops 819200 | bytes 2458400 | tf_op jit(solution)/shard_map/convert_element_type | solution.py:34
  75.1 34.8 %reduce-scatter.2.cloned.1.call-done = bf16[256,200]{0,1:T(8,128)(2,1)} async-done(((bf16[2048,200]{0,1:T(8,128)(2,1)}), bf16[256,200]{0,1:T(8,128)(2,1)}) %reduce-scatter.2.cloned.1.call-update) | async-done | bytes 102416 | tf_op jit(solution)/shard_map/reduce_scatter | solution.py:38
  110.0 1.6 %bitcast_convert_fusion = f32[1,256,200]{1,2,0:T(8,128)} fusion(bf16[256,200]{0,1:T(8,128)(2,1)} %reduce-scatter.2.cloned.1.call-done), kind=kLoop, calls=%fused_computation.13 | loop fusion | flops 51200 | bytes 307200 | tf_op jit(solution)/shard_map/broadcast_in_dim | solution.py:39
Async XLA Ops:
  7.2 46.8 %copy-start = (bf16[512,2048]{1,0:T(8,128)(2,1)S(1)}, bf16[512,2048]{1,0:T(8,128)(2,1)}, u32[]{:S(2)}) copy-start(bf16[512,2048]{1,0:T(8,128)(2,1)} %param.6) | copy-start | bytes 6291460
  7.2 102.8 %reduce-scatter.2.cloned.1.call-start = ((), (), s32[]{:S(2)}) async-start(), calls=%async_computation.2 | async-start | bytes 921600 | tf_op jit(solution)/shard_map/reduce_scatter | solution.py:38
  54.0 6.4 %copy-start.2 = (bf16[1,2048,200]{1,2,0:T(8,128)(2,1)S(1)}, bf16[1,2048,200]{1,2,0:T(8,128)(2,1)}, u32[]{:S(2)}) copy-start(bf16[1,2048,200]{1,2,0:T(8,128)(2,1)} %param.8) | copy-start | bytes 2457604
  60.4 4.0 %copy-start.4 = (bf16[128,16,2048]{2,0,1:T(8,128)(2,1)}, bf16[128,16,2048]{2,0,1:T(8,128)(2,1)S(1)}, u32[]{:S(2)}) copy-start(bf16[128,16,2048]{2,0,1:T(8,128)(2,1)S(1)} %tanh_convert_fusion) | copy-start | bytes 25165828
  60.4 4.0 %copy-start.1 = (f32[1,200]{1,0:T(1,128)S(1)}, f32[1,200]{1,0:T(1,128)}, u32[]{:S(2)}) copy-start(f32[1,200]{1,0:T(1,128)} %param.9) | copy-start | bytes 2404
  60.4 4.0 %copy-start.3 = (bf16[512,200]{0,1:T(8,128)(2,1)S(1)}, bf16[512,200]{0,1:T(8,128)(2,1)}, u32[]{:S(2)}) copy-start(bf16[512,200]{0,1:T(8,128)(2,1)} %param.7) | copy-start | bytes 614404
Sparse Core Ops, SparseCore 0:
  72.7 37.1 reduce-scatter.1

commit v2 on v1

v2 whole, which is shorter than its diff:
```python
import functools
import math

import jax
import jax.numpy as jnp
from jax import lax
from jax.experimental import pallas as pl
from jax.experimental.pallas import tpu as pltpu
from jax.sharding import PartitionSpec as P

MESH = pl.DeviceIdType.MESH
GROUP = 4


def near_first(x, y, z):
    steps = [(dx, dy, dz) for dx in range(x) for dy in range(y) for dz in range(z)]
    return sorted(steps, key=lambda s: min(s[0], x - s[0]) + min(s[1], y - s[1]) + s[2])


def dot_nt(a, b):
    return lax.dot_general(a, b, (((1,), (1,)), ((), ())), preferred_element_type=jnp.float32)


def kernel(
    row_scale,
    f_ref, ld_ref, mp_ref, w_ref, b_ref,
    dec_ref, grad_ref,
    recv, ld, mp, w, bias, feats_a, feats_b, slopes_a, slopes_b, acc, disp, dec_buf,
    s1_send, s1_recv, s2_send, s2_recv, keep,
    load_sem, own_sem, a2a_send, a2a_recv, dec_sem, s1_sems, s1_rsems, s2_sems, s2_rsems,
):
    feats, slopes_t = (feats_a, feats_b), (slopes_a, slopes_b)
    blk = lax.axis_index("blk")
    grp = lax.axis_index("grp")
    path_dev, _, width_k = f_ref.shape
    blocks, _, hour_blk, _ = recv.shape
    share = path_dev * hour_blk
    width_f = ld_ref.shape[1]
    regions = mp_ref.shape[0]
    chunk = 256
    zh, core = grp // 2, grp % 2
    x, y, zl = blk // 8, (blk // 2) % 4, blk % 2
    steps = near_first(4, 4, 2)

    def across(step, sign):
        dx, dy, dz = step
        return (
            ((x + sign * dx + 4) % 4) * 8
            + ((y + sign * dy + 4) % 4) * 2
            + (1 - zl if dz else zl)
        )

    targets = [across(step, 1) for step in steps]
    sources = [across(step, -1) for step in steps]
    partner = (zh * 2 + 1 - core, blk)
    right = (((zh + 1) % 4) * 2 + core, blk)
    left = (((zh + 3) % 4) * 2 + core, blk)

    barrier = pltpu.get_barrier_semaphore()
    givers = [(grp, source) for source in sources[1:]] + [partner, right, left]
    for giver in givers:
        pl.semaphore_signal(barrier, inc=1, device_id=giver, device_id_type=MESH)

    def hours_of(owner):
        return f_ref.at[:, pl.ds(pl.multiple_of(owner * hour_blk, hour_blk), hour_blk), :]

    loads = [
        pltpu.make_async_copy(ld_ref, ld, load_sem.at[0]),
        pltpu.make_async_copy(mp_ref, mp, load_sem.at[1]),
        pltpu.make_async_copy(w_ref.at[0], w, load_sem.at[2]),
        pltpu.make_async_copy(b_ref, bias, load_sem.at[3]),
        pltpu.make_async_copy(hours_of(blk), recv.at[0], own_sem),
    ]
    for load in loads:
        load.start()
    acc[...] = jnp.zeros_like(acc)
    pl.semaphore_wait(barrier, len(givers))

    sends = [
        pltpu.make_async_remote_copy(
            src_ref=hours_of(targets[slot]),
            dst_ref=recv.at[slot],
            send_sem=a2a_send.at[slot],
            recv_sem=a2a_recv.at[slot],
            device_id=(grp, targets[slot]),
            device_id_type=MESH,
        )
        for slot in range(1, blocks)
    ]
    for send in sends:
        send.start()
    for load in loads:
        load.wait()

    def arrived(slot):
        pltpu.make_async_remote_copy(
            src_ref=recv.at[slot], dst_ref=recv.at[slot], send_sem=a2a_send.at[0],
            recv_sem=a2a_recv.at[slot], device_id=partner, device_id_type=MESH,
        ).wait_recv()

    rows = GROUP * share

    def grad_of(at, side):
        part = pl.ds(pl.multiple_of(at, chunk), chunk)
        return acc[:, part] + jnp.dot(
            slopes_t[side][...], feats[side][:, part], preferred_element_type=jnp.float32
        )

    def decide(first, places, side, add_last):
        shocks = recv[pl.ds(first, GROUP)].reshape(rows, width_k)
        for at in range(0, width_f, chunk):
            feats[side][:, at : at + chunk] = jnp.tanh(
                jnp.dot(shocks, ld[:, at : at + chunk], preferred_element_type=jnp.float32)
            ).astype(jnp.bfloat16)
        net = dot_nt(shocks, mp[...])
        dispatch = jnp.broadcast_to(bias[...], (rows, regions))
        for at in range(0, width_f, chunk):
            dispatch = dispatch + dot_nt(feats[side][:, at : at + chunk], w[:, at : at + chunk])
            if add_last:
                acc[:, at : at + chunk] = grad_of(at, 1 - side)
        for i, place in enumerate(places):
            at = pl.multiple_of(place * share, share)
            for col in range(0, regions, 128):
                width = min(128, regions - col)
                disp[col // 128, pl.ds(at, share), :width] = dispatch[
                    i * share : (i + 1) * share, col : col + width
                ]
        shortfall = net.astype(jnp.bfloat16).astype(jnp.float32) - dispatch
        slopes = -1.5 - 2.5 * jnp.tanh(0.5 * shortfall) + 0.25 * dispatch
        slopes_t[side][...] = slopes.T.astype(jnp.bfloat16)

    side = 0
    for first in range(0, blocks, GROUP):
        side = (first // GROUP) % 2
        for slot in range(max(first, 1), first + GROUP):
            arrived(slot)
        decide(first, sources[first : first + GROUP], side, first > 0)

    turns = (2, 1, 3, 0)

    def slice_of(turn, at):
        return grad_of(((zh + turn) % 4) * (2 * chunk) + at * chunk, side)

    swaps = []
    for k, turn in enumerate(turns):
        s1_send[k] = slice_of(turn, 1 - core).astype(jnp.bfloat16)
        swaps.append(
            pltpu.make_async_remote_copy(
                src_ref=s1_send.at[k], dst_ref=s1_recv.at[k], send_sem=s1_sems.at[k],
                recv_sem=s1_rsems.at[k], device_id=partner, device_id_type=MESH,
            )
        )
        swaps[k].start()

    def hop(slot, to):
        return pltpu.make_async_remote_copy(
            src_ref=s2_send.at[slot], dst_ref=s2_recv.at[slot], send_sem=s2_sems.at[slot],
            recv_sem=s2_rsems.at[slot], device_id=to, device_id_type=MESH,
        )

    half = chunk // 2
    moves = [hop(0, right), hop(1, left), hop(2, right), hop(3, right), hop(4, left), hop(5, left)]

    def summed(k):
        value = slice_of(turns[k], core)
        swaps[k].wait_recv()
        return value + s1_recv[k].astype(jnp.float32)

    far = summed(0)
    s2_send[0] = far[:, :half].astype(jnp.bfloat16)
    moves[0].start()
    s2_send[1] = far[:, half:].astype(jnp.bfloat16)
    moves[1].start()
    ahead = summed(1)
    s2_send[3] = ahead[:, half:].astype(jnp.bfloat16)
    moves[3].start()
    keep[0] = ahead[:, :half]
    behind = summed(2)
    s2_send[4] = behind[:, :half].astype(jnp.bfloat16)
    moves[4].start()
    keep[1] = behind[:, half:]
    mine = summed(3)
    keep[2] = mine[:, :half]
    keep[3] = mine[:, half:]

    for hour in range(hour_blk):
        for side in range(0, regions, 128):
            width = min(128, regions - side)
            of_hour = disp[side // 128, pl.ds(hour, blocks * path_dev, stride=hour_blk), :]
            dec_buf[hour, side : side + width] = of_hour.T[:width].astype(jnp.bfloat16)
    out = pltpu.make_async_copy(dec_buf, dec_ref, dec_sem)
    out.start()

    moves[0].wait_recv()
    s2_send[2] = (keep[0] + s2_recv[0].astype(jnp.float32)).astype(jnp.bfloat16)
    moves[2].start()
    moves[1].wait_recv()
    s2_send[5] = (keep[1] + s2_recv[1].astype(jnp.float32)).astype(jnp.bfloat16)
    moves[5].start()
    for k in range(2, 6):
        moves[k].wait_recv()
    for k in range(2):
        total = keep[2 + k] + s2_recv[2 + k].astype(jnp.float32) + s2_recv[4 + k].astype(jnp.float32)
        grad_ref[0, :, k * half : (k + 1) * half] = total * row_scale

    out.wait()
    for copy in sends + swaps + moves:
        copy.wait_send()


def body(factors, loadings, netload_map, rule_weights, rule_bias):
    blocks = lax.axis_size("blk")
    grps = lax.axis_size("grp")
    path_dev, hours, width_k = factors.shape
    width_f, regions = rule_weights.shape[1:]
    hour_blk = hours // blocks
    row_scale = 1.0 / math.sqrt(grps * blocks * path_dev * hour_blk)
    share = path_dev * hour_blk
    owned = width_f // grps
    bf16, f32 = jnp.bfloat16, jnp.float32
    anywhere = pl.BlockSpec(memory_space=pl.ANY)
    dma = pltpu.SemaphoreType.DMA
    decisions_t, grad_t = pl.pallas_call(
        functools.partial(kernel, row_scale),
        out_shape=(
            jax.ShapeDtypeStruct((hour_blk, regions, blocks * path_dev), bf16),
            jax.ShapeDtypeStruct((1, regions, owned), f32),
        ),
        in_specs=[anywhere] * 5,
        out_specs=(anywhere, pl.BlockSpec(memory_space=pltpu.VMEM)),
        scratch_shapes=[
            pltpu.VMEM((blocks, path_dev, hour_blk, width_k), bf16),
            pltpu.VMEM(loadings.shape, bf16),
            pltpu.VMEM((regions, width_k), bf16),
            pltpu.VMEM((regions, width_f), bf16),
            pltpu.VMEM((1, regions), f32),
            pltpu.VMEM((GROUP * share, width_f), bf16),
            pltpu.VMEM((GROUP * share, width_f), bf16),
            pltpu.VMEM((regions, GROUP * share), bf16),
            pltpu.VMEM((regions, GROUP * share), bf16),
            pltpu.VMEM((regions, width_f), f32),
            pltpu.VMEM((-(-regions // 128), blocks * share, 128), f32),
            pltpu.VMEM((hour_blk, regions, blocks * path_dev), bf16),
            pltpu.VMEM((4, regions, owned), bf16),
            pltpu.VMEM((4, regions, owned), bf16),
            pltpu.VMEM((6, regions, owned // 2), bf16),
            pltpu.VMEM((6, regions, owned // 2), bf16),
            pltpu.VMEM((4, regions, owned // 2), f32),
            dma((4,)),
            dma,
            dma((blocks,)),
            dma((blocks,)),
            dma,
            dma((4,)),
            dma((4,)),
            dma((6,)),
            dma((6,)),
        ],
        compiler_params=pltpu.CompilerParams(
            collective_id=0, has_side_effects=True, vmem_limit_bytes=56 * 1024 * 1024
        ),
        name="exchange_decide_reduce",
    )(factors, loadings, netload_map.T, jnp.swapaxes(rule_weights, 1, 2), rule_bias)
    return jnp.swapaxes(decisions_t, 1, 2), jnp.swapaxes(grad_t, 1, 2)


def solution(mesh):
    return jax.shard_map(
        body,
        mesh=mesh,
        in_specs=(P(("grp", "blk"), None, None), P(), P(), P("blk", None, None), P("blk", None)),
        out_specs=(P("blk", "grp", None), P("blk", "grp", None)),
        check_vma=False,
    )
```

time: 119 us -> 59.5 us (0.50)
  Pallas kernels: 0 us -> 55 us
  blocking collectives: 37.1 us -> 0 us
  waiting for transfers between devices: 34.8 us -> 0 us
  matrix products: 18.5 us -> 0 us
  between operations: 14.1 us -> 0.64 us
  local copies, waits for them, and re-layouts: 9.72 us -> 3.71 us
  other arithmetic: 4.11 us -> 0 us
    pallas_call x0 -> x1, Pallas kernels: none -> 55 us  [body(): pl.pallas_call(functools.partial(kernel, row_scale), out_shape=(jax.Shape...]
    all_to_all x1 -> x0, blocking collectives: 37.1 us -> none  [body(): lax.all_to_all(ordered, 'blk', split_axis=1, concat_axis=0, tiled=True)]
    reduce_scatter x1 -> x0, waiting for transfers between devices: 34.8 us -> none  [body(): lax.psum_scatter(partial_grad, 'grp', scatter_dimension=0, tiled=True)]
    dot_general x3 -> x0, matrix products: 18.5 us -> none  [the longest x1 8.15 us: body(): jnp.einsum('rkf,rkd->fd', features, slopes, preferred_element_type=jnp.fl...]
    reshape x1 -> x0, local copies, waits for them, and re-layouts: 3.98 us -> none  [body(): shocks = shocks.reshape(blocks * path_dev, hour_blk, width_k)]
    convert_element_type x1 -> x0, other arithmetic: 2.52 us -> none  [body(): decisions = jnp.transpose(dispatch.astype(jnp.bfloat16), (1, 0, 2))]
    all_to_all x1 -> x0, local copies, waits for them, and re-layouts: 2.35 us -> none  [body(): lax.all_to_all(ordered, 'blk', split_axis=1, concat_axis=0, tiled=True)]
    broadcast_in_dim x1 -> x0, other arithmetic: 1.59 us -> none  [body(): return (decisions, grad_share.astype(jnp.float32)[None])]
  transfers between devices with their start and end apart: 1 -> 0, of which waited for: 1 -> 0; matrix products, arithmetic and copies ran while one was open for 2% -> 0% of each run, Pallas kernels for 0% -> 0%
where the time goes in v2:
time: 59.5 us; the launch traced here: 59.4 us
  Pallas kernels  55 us (92%)
  local copies, waits for them, and re-layouts  3.71 us (6%)
  between operations  0.64 us (1%)
    pallas_call x1, Pallas kernels, body(): pl.pallas_call(functools.partial(kernel, row_scale), out_shape=(jax.Shape...  55 us
    unnamed x2, local copies, waits for them, and re-layouts  3.71 us

profile of v2, /device:TPU:1, one launch (start us, length us, event | category | flops | bytes accessed | tf_op | source)
XLA Modules:
  0.0 59.4 jit_solution(5151364660712875834)
XLA Ops:
  0.6 55.0 %exchange_decide_reduce.1 = (bf16[16,200,128]{2,1,0:T(8,128)(2,1)}, f32[1,200,256]{2,1,0:T(8,128)}) custom-call(bf16[4,512,512]{2,1,0:T(8,128)(2,1)} %f_ref.1, bf16[512,2048]{1,0:T(8,128)(2,1)} %ld_ref.1, bf16[200,512]{1,0:T(8,128)(2,1)} %bitcast.7, bf16[1,200,2048]{2,1,0:T(8,128)(2,1)} %bitcast.5, f32[1,200]{1,0:T(1,128)} %b_ref.1), custom_call_target="tpu_custom_call" | custom-call | tf_op jit(solution)/shard_map/exchange_decide_reduce/pallas_call | solution.py:223
  55.7 2.1 %copy.9 = bf16[16,128,200]{1,2,0:T(8,128)(2,1)} copy(bf16[16,128,200]{1,2,0:T(8,128)(2,1)} %bitcast.4) | data formatting | bytes 1638400
  57.8 1.6 %copy.10 = f32[1,256,200]{1,2,0:T(8,128)} copy(f32[1,256,200]{1,2,0:T(8,128)} %bitcast.6) | data formatting | bytes 409600

commit v3 on v2

--- a/solution.py
+++ b/solution.py
@@ -12,9 +12,23 @@
 GROUP = 4
 
 
-def near_first(x, y, z):
-    steps = [(dx, dy, dz) for dx in range(x) for dy in range(y) for dz in range(z)]
-    return sorted(steps, key=lambda s: min(s[0], x - s[0]) + min(s[1], y - s[1]) + s[2])
+STEPS = (
+    (0, 0, 0), (0, 0, 1), (1, 0, 0), (3, 0, 0),
+    (1, 0, 1), (1, 1, 0), (1, 3, 0), (2, 0, 0),
+    (3, 0, 1), (3, 1, 0), (3, 3, 0), (1, 1, 1),
+    (1, 3, 1), (2, 0, 1), (0, 1, 0), (0, 3, 0),
+    (0, 1, 1), (0, 2, 0), (0, 3, 1), (2, 1, 0),
+    (2, 3, 0), (3, 1, 1), (3, 3, 1), (0, 2, 1),
+    (1, 2, 1), (2, 1, 1), (1, 2, 0), (3, 2, 0),
+    (2, 2, 0), (2, 3, 1), (3, 2, 1), (2, 2, 1),
+)
+
+
+def hops(step):
+    return min(step[0], 4 - step[0]) + min(step[1], 4 - step[1]) + step[2]
+
+
+SEND_ORDER = sorted(range(1, len(STEPS)), key=lambda slot: (hops(STEPS[slot]), STEPS[slot]))
 
 
 def dot_nt(a, b):
@@ -25,9 +39,9 @@
     row_scale,
     f_ref, ld_ref, mp_ref, w_ref, b_ref,
     dec_ref, grad_ref,
-    recv, ld, mp, w, bias, feats_a, feats_b, slopes_a, slopes_b, acc, disp, dec_buf,
+    recv, ld, mp, w, bias, feats_a, feats_b, slopes_a, slopes_b, acc, disp,
     s1_send, s1_recv, s2_send, s2_recv, keep,
-    load_sem, own_sem, a2a_send, a2a_recv, dec_sem, s1_sems, s1_rsems, s2_sems, s2_rsems,
+    load_sem, own_sem, a2a_send, a2a_recv, s1_sems, s1_rsems, s2_sems, s2_rsems,
 ):
     feats, slopes_t = (feats_a, feats_b), (slopes_a, slopes_b)
     blk = lax.axis_index("blk")
@@ -40,7 +54,6 @@
     chunk = 256
     zh, core = grp // 2, grp % 2
     x, y, zl = blk // 8, (blk // 2) % 4, blk % 2
-    steps = near_first(4, 4, 2)
 
     def across(step, sign):
         dx, dy, dz = step
@@ -50,8 +63,8 @@
             + (1 - zl if dz else zl)
         )
 
-    targets = [across(step, 1) for step in steps]
-    sources = [across(step, -1) for step in steps]
+    targets = [across(step, 1) for step in STEPS]
+    sources = [across(step, -1) for step in STEPS]
     partner = (zh * 2 + 1 - core, blk)
     right = (((zh + 1) % 4) * 2 + core, blk)
     left = (((zh + 3) % 4) * 2 + core, blk)
@@ -76,8 +89,8 @@
     acc[...] = jnp.zeros_like(acc)
     pl.semaphore_wait(barrier, len(givers))
 
-    sends = [
-        pltpu.make_async_remote_copy(
+    sends = {
+        slot: pltpu.make_async_remote_copy(
             src_ref=hours_of(targets[slot]),
             dst_ref=recv.at[slot],
             send_sem=a2a_send.at[slot],
@@ -85,10 +98,10 @@
             device_id=(grp, targets[slot]),
             device_id_type=MESH,
         )
-        for slot in range(1, blocks)
-    ]
-    for send in sends:
-        send.start()
+        for slot in SEND_ORDER
+    }
+    for slot in SEND_ORDER:
+        sends[slot].start()
     for load in loads:
         load.wait()
 
@@ -173,12 +186,14 @@
     moves[1].start()
     ahead = summed(1)
     s2_send[3] = ahead[:, half:].astype(jnp.bfloat16)
-    moves[3].start()
     keep[0] = ahead[:, :half]
     behind = summed(2)
     s2_send[4] = behind[:, :half].astype(jnp.bfloat16)
+    keep[1] = behind[:, half:]
+    moves[0].wait_send()
+    moves[3].start()
+    moves[1].wait_send()
     moves[4].start()
-    keep[1] = behind[:, half:]
     mine = summed(3)
     keep[2] = mine[:, :half]
     keep[3] = mine[:, half:]
@@ -187,9 +202,7 @@
         for side in range(0, regions, 128):
             width = min(128, regions - side)
             of_hour = disp[side // 128, pl.ds(hour, blocks * path_dev, stride=hour_blk), :]
-            dec_buf[hour, side : side + width] = of_hour.T[:width].astype(jnp.bfloat16)
-    out = pltpu.make_async_copy(dec_buf, dec_ref, dec_sem)
-    out.start()
+            dec_ref[hour, side : side + width] = of_hour.T[:width].astype(jnp.bfloat16)
 
     moves[0].wait_recv()
     s2_send[2] = (keep[0] + s2_recv[0].astype(jnp.float32)).astype(jnp.bfloat16)
@@ -203,9 +216,19 @@
         total = keep[2 + k] + s2_recv[2 + k].astype(jnp.float32) + s2_recv[4 + k].astype(jnp.float32)
         grad_ref[0, :, k * half : (k + 1) * half] = total * row_scale
 
-    out.wait()
-    for copy in sends + swaps + moves:
+    for copy in list(sends.values()) + swaps + moves[2:]:
         copy.wait_send()
+
+
+def write_out(dec_ref, grad_ref, dec_out, grad_out, sems):
+    copies = [
+        pltpu.make_async_copy(dec_ref, dec_out, sems.at[0]),
+        pltpu.make_async_copy(grad_ref, grad_out, sems.at[1]),
+    ]
+    for copy in copies:
+        copy.start()
+    for copy in copies:
+        copy.wait()
 
 
 def body(factors, loadings, netload_map, rule_weights, rule_bias):
@@ -219,15 +242,16 @@
     owned = width_f // grps
     bf16, f32 = jnp.bfloat16, jnp.float32
     anywhere = pl.BlockSpec(memory_space=pl.ANY)
+    vmem = pl.BlockSpec(memory_space=pltpu.VMEM)
     dma = pltpu.SemaphoreType.DMA
     decisions_t, grad_t = pl.pallas_call(
         functools.partial(kernel, row_scale),
         out_shape=(
-            jax.ShapeDtypeStruct((hour_blk, regions, blocks * path_dev), bf16),
-            jax.ShapeDtypeStruct((1, regions, owned), f32),
+            pltpu.VMEM((hour_blk, regions, blocks * path_dev), bf16),
+            pltpu.VMEM((1, regions, owned), f32),
         ),
         in_specs=[anywhere] * 5,
-        out_specs=(anywhere, pl.BlockSpec(memory_space=pltpu.VMEM)),
+        out_specs=(vmem, vmem),
         scratch_shapes=[
             pltpu.VMEM((blocks, path_dev, hour_blk, width_k), bf16),
             pltpu.VMEM(loadings.shape, bf16),
@@ -240,7 +264,6 @@
             pltpu.VMEM((regions, GROUP * share), bf16),
             pltpu.VMEM((regions, width_f), f32),
             pltpu.VMEM((-(-regions // 128), blocks * share, 128), f32),
-            pltpu.VMEM((hour_blk, regions, blocks * path_dev), bf16),
             pltpu.VMEM((4, regions, owned), bf16),
             pltpu.VMEM((4, regions, owned), bf16),
             pltpu.VMEM((6, regions, owned // 2), bf16),
@@ -250,7 +273,6 @@
             dma,
             dma((blocks,)),
             dma((blocks,)),
-            dma,
             dma((4,)),
             dma((4,)),
             dma((6,)),
@@ -261,6 +283,17 @@
         ),
         name="exchange_decide_reduce",
     )(factors, loadings, netload_map.T, jnp.swapaxes(rule_weights, 1, 2), rule_bias)
+    decisions_t, grad_t = pl.pallas_call(
+        write_out,
+        out_shape=(
+            jax.ShapeDtypeStruct(decisions_t.shape, bf16),
+            jax.ShapeDtypeStruct(grad_t.shape, f32),
+        ),
+        in_specs=[vmem, vmem],
+        out_specs=(anywhere, anywhere),
+        scratch_shapes=[dma((2,))],
+        name="write_out",
+    )(*(pltpu.with_memory_space_constraint(a, pltpu.VMEM) for a in (decisions_t, grad_t)))
     return jnp.swapaxes(decisions_t, 1, 2), jnp.swapaxes(grad_t, 1, 2)
 
 

time: 59.5 us -> 52.6 us (0.88)
  local copies, waits for them, and re-layouts: 3.71 us -> 0 us
  Pallas kernels: 55 us -> 51.8 us
    unnamed x2 -> x0, local copies, waits for them, and re-layouts: 3.71 us -> none
    pallas_call x1 -> x2, Pallas kernels: 55 us -> 51.8 us  [the longest x1 50.9 us: body(): pl.pallas_call(functools.partial(kernel, row_scale), out_shape=(pltpu.VME...]
where the time goes in v3:
time: 52.6 us; the launch traced here: 52.5 us
  Pallas kernels  51.8 us (98%)
  between operations  0.64 us (1%)
    pallas_call x1, Pallas kernels, body(): pl.pallas_call(functools.partial(kernel, row_scale), out_shape=(pltpu.VME...  50.9 us

profile of v3, /device:TPU:1, one launch (start us, length us, event | category | flops | bytes accessed | tf_op | source)
XLA Modules:
  0.0 52.5 jit_solution(2846718634609218358)
XLA Ops:
  0.6 50.9 %exchange_decide_reduce.1 = (bf16[16,200,128]{2,1,0:T(8,128)(2,1)S(1)}, f32[1,200,256]{2,1,0:T(8,128)S(1)}) custom-call(bf16[4,512,512]{2,1,0:T(8,128)(2,1)} %f_ref.1, bf16[512,2048]{1,0:T(8,128)(2,1)} %ld_ref.1, bf16[200,512]{1,0:T(8,128)(2,1)} %bitcast.5, bf16[1,200,2048]{2,1,0:T(8,128)(2,1)} %bitcast.4, f32[1,200]{1,0:T(1,128)} %b_ref.1), custom_call_target="tpu_custom_call" | custom-call | tf_op jit(solution)/shard_map/exchange_decide_reduce/pallas_call | solution.py:247
  51.5 1.0 %write_out.1 = (bf16[16,200,128]{2,1,0:T(8,128)(2,1)}, f32[1,200,256]{2,1,0:T(8,128)}) custom-call(bf16[16,200,128]{2,1,0:T(8,128)(2,1)S(1)} %get-tuple-element.6.dec_ref, f32[1,200,256]{2,1,0:T(8,128)S(1)} %get-tuple-element.7.grad_ref), custom_call_target="tpu_custom_call" | custom-call | tf_op jit(solution)/shard_map/write_out/pallas_call | solution.py:286

commit v4 on v3

--- a/solution.py
+++ b/solution.py
@@ -41,7 +41,7 @@
     dec_ref, grad_ref,
     recv, ld, mp, w, bias, feats_a, feats_b, slopes_a, slopes_b, acc, disp,
     s1_send, s1_recv, s2_send, s2_recv, keep,
-    load_sem, own_sem, a2a_send, a2a_recv, s1_sems, s1_rsems, s2_sems, s2_rsems,
+    rounds, load_sem, own_sem, a2a_send, a2a_recv, s1_sems, s1_rsems, s2_sems, s2_rsems,
 ):
     feats, slopes_t = (feats_a, feats_b), (slopes_a, slopes_b)
     blk = lax.axis_index("blk")
@@ -63,16 +63,18 @@
             + (1 - zl if dz else zl)
         )
 
-    targets = [across(step, 1) for step in STEPS]
-    sources = [across(step, -1) for step in STEPS]
     partner = (zh * 2 + 1 - core, blk)
     right = (((zh + 1) % 4) * 2 + core, blk)
     left = (((zh + 3) % 4) * 2 + core, blk)
 
     barrier = pltpu.get_barrier_semaphore()
-    givers = [(grp, source) for source in sources[1:]] + [partner, right, left]
-    for giver in givers:
-        pl.semaphore_signal(barrier, inc=1, device_id=giver, device_id_type=MESH)
+    around = [(grp, across(STEPS[slot], 1)) for slot in SEND_ORDER if hops(STEPS[slot]) == 1]
+    greeted = around + [partner, right, left]
+    for device in greeted:
+        pl.semaphore_signal(barrier, inc=1, device_id=device, device_id_type=MESH)
+
+    targets = [across(step, 1) for step in STEPS]
+    sources = [across(step, -1) for step in STEPS]
 
     def hours_of(owner):
         return f_ref.at[:, pl.ds(pl.multiple_of(owner * hour_blk, hour_blk), hour_blk), :]
@@ -86,8 +88,7 @@
     ]
     for load in loads:
         load.start()
-    acc[...] = jnp.zeros_like(acc)
-    pl.semaphore_wait(barrier, len(givers))
+    pl.semaphore_wait(barrier, len(greeted))
 
     sends = {
         slot: pltpu.make_async_remote_copy(
@@ -100,8 +101,18 @@
         )
         for slot in SEND_ORDER
     }
-    for slot in SEND_ORDER:
-        sends[slot].start()
+    farthest = hops(STEPS[SEND_ORDER[-1]])
+    for reach in range(1, farthest + 1):
+        if reach > 1:
+            pl.semaphore_wait(rounds.at[reach], len(around))
+        if reach < farthest:
+            for device in around:
+                pl.semaphore_signal(
+                    rounds.at[reach + 1], inc=1, device_id=device, device_id_type=MESH
+                )
+        for slot in SEND_ORDER:
+            if hops(STEPS[slot]) == reach:
+                sends[slot].start()
     for load in loads:
         load.wait()
 
@@ -113,13 +124,14 @@
 
     rows = GROUP * share
 
-    def grad_of(at, side):
+    def grad_of(at, side, add=True):
         part = pl.ds(pl.multiple_of(at, chunk), chunk)
-        return acc[:, part] + jnp.dot(
+        value = jnp.dot(
             slopes_t[side][...], feats[side][:, part], preferred_element_type=jnp.float32
         )
-
-    def decide(first, places, side, add_last):
+        return acc[:, part] + value if add else value
+
+    def decide(first, places, side, add):
         shocks = recv[pl.ds(first, GROUP)].reshape(rows, width_k)
         for at in range(0, width_f, chunk):
             feats[side][:, at : at + chunk] = jnp.tanh(
@@ -129,8 +141,8 @@
         dispatch = jnp.broadcast_to(bias[...], (rows, regions))
         for at in range(0, width_f, chunk):
             dispatch = dispatch + dot_nt(feats[side][:, at : at + chunk], w[:, at : at + chunk])
-            if add_last:
-                acc[:, at : at + chunk] = grad_of(at, 1 - side)
+            if add is not None:
+                acc[:, at : at + chunk] = grad_of(at, 1 - side, add)
         for i, place in enumerate(places):
             at = pl.multiple_of(place * share, share)
             for col in range(0, regions, 128):
@@ -147,7 +159,7 @@
         side = (first // GROUP) % 2
         for slot in range(max(first, 1), first + GROUP):
             arrived(slot)
-        decide(first, sources[first : first + GROUP], side, first > 0)
+        decide(first, sources[first : first + GROUP], side, first > GROUP if first else None)
 
     turns = (2, 1, 3, 0)
 
@@ -269,6 +281,7 @@
             pltpu.VMEM((6, regions, owned // 2), bf16),
             pltpu.VMEM((6, regions, owned // 2), bf16),
             pltpu.VMEM((4, regions, owned // 2), f32),
+            pltpu.SemaphoreType.REGULAR((6,)),
             dma((4,)),
             dma,
             dma((blocks,)),

time: 52.6 us -> 50.4 us (0.958)
  Pallas kernels: 51.8 us -> 49.7 us
    pallas_call x1, Pallas kernels: 50.9 us -> 48.8 us  [body(): pl.pallas_call(functools.partial(kernel, row_scale), out_shape=(pltpu.VME...]
where the time goes in v4:
time: 50.4 us
  Pallas kernels  49.7 us (99%)
  between operations  0.64 us (1%)
    pallas_call x1, Pallas kernels, body(): pl.pallas_call(functools.partial(kernel, row_scale), out_shape=(pltpu.VME...  48.8 us

profile of v4, /device:TPU:1, one launch (start us, length us, event | category | flops | bytes accessed | tf_op | source)
XLA Modules:
  0.0 50.4 jit_solution(11565819384545047274)
XLA Ops:
  0.6 48.8 %exchange_decide_reduce.1 = (bf16[16,200,128]{2,1,0:T(8,128)(2,1)S(1)}, f32[1,200,256]{2,1,0:T(8,128)S(1)}) custom-call(bf16[4,512,512]{2,1,0:T(8,128)(2,1)} %f_ref.1, bf16[512,2048]{1,0:T(8,128)(2,1)} %ld_ref.1, bf16[200,512]{1,0:T(8,128)(2,1)} %bitcast.5, bf16[1,200,2048]{2,1,0:T(8,128)(2,1)} %bitcast.4, f32[1,200]{1,0:T(1,128)} %b_ref.1), custom_call_target="tpu_custom_call" | custom-call | tf_op jit(solution)/shard_map/exchange_decide_reduce/pallas_call | solution.py:259
  49.4 1.0 %write_out.1 = (bf16[16,200,128]{2,1,0:T(8,128)(2,1)}, f32[1,200,256]{2,1,0:T(8,128)}) custom-call(bf16[16,200,128]{2,1,0:T(8,128)(2,1)S(1)} %get-tuple-element.6.dec_ref, f32[1,200,256]{2,1,0:T(8,128)S(1)} %get-tuple-element.7.grad_ref), custom_call_target="tpu_custom_call" | custom-call | tf_op jit(solution)/shard_map/write_out/pallas_call | solution.py:299

commit v5 on v4

--- a/solution.py
+++ b/solution.py
@@ -9,7 +9,7 @@
 from jax.sharding import PartitionSpec as P
 
 MESH = pl.DeviceIdType.MESH
-GROUP = 4
+BATCHES = (4, 4, 4, 4, 4, 4, 4, 2, 2)
 
 
 STEPS = (
@@ -122,27 +122,27 @@
             recv_sem=a2a_recv.at[slot], device_id=partner, device_id_type=MESH,
         ).wait_recv()
 
-    rows = GROUP * share
-
-    def grad_of(at, side, add=True):
+
+    def grad_of(at, side, rows, add=True):
         part = pl.ds(pl.multiple_of(at, chunk), chunk)
         value = jnp.dot(
-            slopes_t[side][...], feats[side][:, part], preferred_element_type=jnp.float32
+            slopes_t[side][:, :rows], feats[side][:rows, part], preferred_element_type=jnp.float32
         )
         return acc[:, part] + value if add else value
 
-    def decide(first, places, side, add):
-        shocks = recv[pl.ds(first, GROUP)].reshape(rows, width_k)
+    def decide(first, places, side, before, add):
+        rows = len(places) * share
+        shocks = recv[pl.ds(first, len(places))].reshape(rows, width_k)
         for at in range(0, width_f, chunk):
-            feats[side][:, at : at + chunk] = jnp.tanh(
+            feats[side][:rows, at : at + chunk] = jnp.tanh(
                 jnp.dot(shocks, ld[:, at : at + chunk], preferred_element_type=jnp.float32)
             ).astype(jnp.bfloat16)
         net = dot_nt(shocks, mp[...])
         dispatch = jnp.broadcast_to(bias[...], (rows, regions))
         for at in range(0, width_f, chunk):
-            dispatch = dispatch + dot_nt(feats[side][:, at : at + chunk], w[:, at : at + chunk])
-            if add is not None:
-                acc[:, at : at + chunk] = grad_of(at, 1 - side, add)
+            dispatch = dispatch + dot_nt(feats[side][:rows, at : at + chunk], w[:, at : at + chunk])
+            if before:
+                acc[:, at : at + chunk] = grad_of(at, 1 - side, before, add)
         for i, place in enumerate(places):
             at = pl.multiple_of(place * share, share)
             for col in range(0, regions, 128):
@@ -152,19 +152,21 @@
                 ]
         shortfall = net.astype(jnp.bfloat16).astype(jnp.float32) - dispatch
         slopes = -1.5 - 2.5 * jnp.tanh(0.5 * shortfall) + 0.25 * dispatch
-        slopes_t[side][...] = slopes.T.astype(jnp.bfloat16)
-
-    side = 0
-    for first in range(0, blocks, GROUP):
-        side = (first // GROUP) % 2
-        for slot in range(max(first, 1), first + GROUP):
+        slopes_t[side][:, :rows] = slopes.T.astype(jnp.bfloat16)
+
+    first = 0
+    for batch, count in enumerate(BATCHES):
+        side = batch % 2
+        for slot in range(max(first, 1), first + count):
             arrived(slot)
-        decide(first, sources[first : first + GROUP], side, first > GROUP if first else None)
+        before = BATCHES[batch - 1] * share if batch else 0
+        decide(first, sources[first : first + count], side, before, batch > 1)
+        first += count
 
     turns = (2, 1, 3, 0)
 
     def slice_of(turn, at):
-        return grad_of(((zh + turn) % 4) * (2 * chunk) + at * chunk, side)
+        return grad_of(((zh + turn) % 4) * (2 * chunk) + at * chunk, side, BATCHES[-1] * share)
 
     swaps = []
     for k, turn in enumerate(turns):
@@ -270,10 +272,10 @@
             pltpu.VMEM((regions, width_k), bf16),
             pltpu.VMEM((regions, width_f), bf16),
             pltpu.VMEM((1, regions), f32),
-            pltpu.VMEM((GROUP * share, width_f), bf16),
-            pltpu.VMEM((GROUP * share, width_f), bf16),
-            pltpu.VMEM((regions, GROUP * share), bf16),
-            pltpu.VMEM((regions, GROUP * share), bf16),
+            pltpu.VMEM((max(BATCHES) * share, width_f), bf16),
+            pltpu.VMEM((max(BATCHES) * share, width_f), bf16),
+            pltpu.VMEM((regions, max(BATCHES) * share), bf16),
+            pltpu.VMEM((regions, max(BATCHES) * share), bf16),
             pltpu.VMEM((regions, width_f), f32),
             pltpu.VMEM((-(-regions // 128), blocks * share, 128), f32),
             pltpu.VMEM((4, regions, owned), bf16),

time: 50.4 us -> 51.4 us (1.020)
  Pallas kernels: 49.7 us -> 50.7 us
    pallas_call x1, Pallas kernels: 48.8 us -> 49.7 us  [body(): pl.pallas_call(functools.partial(kernel, row_scale), out_shape=(pltpu.VME...]
where the time goes in v5:
time: 51.4 us; the launch traced here: 51.3 us
  Pallas kernels  50.7 us (99%)
  between operations  0.64 us (1%)
    pallas_call x1, Pallas kernels, body(): pl.pallas_call(functools.partial(kernel, row_scale), out_shape=(pltpu.VME...  49.7 us

profile of v5, /device:TPU:1, one launch (start us, length us, event | category | flops | bytes accessed | tf_op | source)
XLA Modules:
  0.0 51.3 jit_solution(7806723120490975054)
XLA Ops:
  0.6 49.7 %exchange_decide_reduce.1 = (bf16[16,200,128]{2,1,0:T(8,128)(2,1)S(1)}, f32[1,200,256]{2,1,0:T(8,128)S(1)}) custom-call(bf16[4,512,512]{2,1,0:T(8,128)(2,1)} %f_ref.1, bf16[512,2048]{1,0:T(8,128)(2,1)} %ld_ref.1, bf16[200,512]{1,0:T(8,128)(2,1)} %bitcast.5, bf16[1,200,2048]{2,1,0:T(8,128)(2,1)} %bitcast.4, f32[1,200]{1,0:T(1,128)} %b_ref.1), custom_call_target="tpu_custom_call" | custom-call | tf_op jit(solution)/shard_map/exchange_decide_reduce/pallas_call | solution.py:261
  50.3 1.0 %write_out.1 = (bf16[16,200,128]{2,1,0:T(8,128)(2,1)}, f32[1,200,256]{2,1,0:T(8,128)}) custom-call(bf16[16,200,128]{2,1,0:T(8,128)(2,1)S(1)} %get-tuple-element.6.dec_ref, f32[1,200,256]{2,1,0:T(8,128)S(1)} %get-tuple-element.7.grad_ref), custom_call_target="tpu_custom_call" | custom-call | tf_op jit(solution)/shard_map/write_out/pallas_call | solution.py:301
